TPU v7x, 256 devices: a whole 4x4x8 slice. The times are simulated.
256 devices in a mesh: tok: 8 (over z), tp: 16 (over y, x), grp: 2 (over core).
Axes of the slice: x: 4, y: 4, z: 8, core: 2. Of those that a mesh axis runs over, the one named last changes fastest.
Arguments:
- hidden: bfloat16 [2048, 6144], P(('tok', 'grp'), 'tp'), may hold values from -6 to 6
- gain: bfloat16 [6144], P('tp'), may hold values from 0.5 to 1.5
- expert_ids: int32 [2048, 2], P(('tok', 'grp')), may hold values from 0 to 7, all different within a row; in each aligned block of 128 rows (0 to 127, 128 to 255, ...) at most 40 rows name the same one
- gate_weights: float32 [2048, 2], P(('tok', 'grp')), may hold values from 0.1 to 0.9
- segment_ids: int32 [2048], P(('tok', 'grp')), may hold values from 0 to 15, never falling along the last dimension, each value on 1 to 384 neighbouring positions
- upstream: bfloat16 [2048, 6144], P(('tok', 'grp'), 'tp'), may hold values from -6 to 6
- w_gate: bfloat16 [8, 6144, 8192], P('tok', None, ('tp', 'grp')), may hold values from -0.078125 to 0.078125
- w_up: bfloat16 [8, 6144, 8192], P('tok', None, ('tp', 'grp')), may hold values from -0.078125 to 0.078125
- w_down: bfloat16 [8, 8192, 6144], P('tok', ('tp', 'grp')), may hold values from -0.0625 to 0.0625
Outputs:
- mixed: bfloat16 [2048, 6144], P(('tok', 'grp'), 'tp')
- importance: float32 [8, 8192], P('tok', ('tp', 'grp'))
Inputs may be any that keep to these rules, and one draw needn't show every extreme that they name: `expert_ids`: each token names 2 different experts. Within the tokens of one token shard (aligned blocks of 128 rows) no expert is named by more than 40 tokens, and in some block one expert is named by exactly 40. `segment_ids`: never falling along the tokens; every document holds between 1 and 384 tokens.
All inputs are finite; a program needn't handle non-finite values.
Results may differ from a plain program's by a relative error of at most 0.0095.
Values may be sent and summed in bfloat16 or wider, within the bound.
No kernel may reach another device: no remote copies, remote signals or barrier semaphores. Data moves between devices by JAX's collectives and lax.ppermute only.
A program may use at most 128 MiB of HBM per device.

v0:
```python
import jax
import jax.numpy as jnp
from jax import lax
from jax.sharding import PartitionSpec as P


def expert_pass(rows_in, cot_in, gate_mat, up_mat, down_mat):
    gate_pre = jnp.dot(rows_in, gate_mat, preferred_element_type=jnp.float32)
    up_proj = jnp.dot(rows_in, up_mat, preferred_element_type=jnp.float32)
    sigmoid_gate = jax.nn.sigmoid(gate_pre)
    activated = gate_pre * sigmoid_gate
    hidden_act = (activated * up_proj).astype(jnp.bfloat16)
    grad_act = lax.dot_general(
        cot_in, down_mat, (((1,), (1,)), ((), ())), preferred_element_type=jnp.float32
    )
    grad_gate = (
        grad_act * up_proj * sigmoid_gate * (1.0 + gate_pre * (1.0 - sigmoid_gate))
    ).astype(jnp.bfloat16)
    grad_up = (grad_act * activated).astype(jnp.bfloat16)
    grad_wgate = lax.dot_general(
        rows_in, grad_gate, (((0,), (0,)), ((), ())), preferred_element_type=jnp.float32
    )
    grad_wup = lax.dot_general(
        rows_in, grad_up, (((0,), (0,)), ((), ())), preferred_element_type=jnp.float32
    )
    grad_wdown = lax.dot_general(
        hidden_act, cot_in, (((0,), (0,)), ((), ())), preferred_element_type=jnp.float32
    )
    scores = jnp.sum(jnp.abs(grad_wgate * gate_mat.astype(jnp.float32)), axis=0)
    scores = scores + jnp.sum(jnp.abs(grad_wup * up_mat.astype(jnp.float32)), axis=0)
    scores = scores + jnp.sum(jnp.abs(grad_wdown * down_mat.astype(jnp.float32)), axis=1)
    return (hidden_act, scores)


def on_device(hidden, gain, expert_ids, gate_weights, segment_ids, upstream, w_gate, w_up, w_down):
    rows_here = hidden.shape[0]
    top_count = expert_ids.shape[1]
    experts = lax.axis_size("tok")
    groups = lax.axis_size("grp")
    capacity = 5 * rows_here // (2 * experts)
    width = w_gate.shape[1]
    documents = jnp.arange(experts * groups, dtype=jnp.int32)
    doc_onehot = (segment_ids[:, None] == documents[None, :]).astype(jnp.float32)
    doc_len = lax.psum(jnp.sum(doc_onehot, axis=0), ("tok", "grp"))
    tok_len = jnp.sum(doc_onehot * doc_len[None, :], axis=1)
    tok_weight = rows_here / tok_len
    onehot = (
        expert_ids.reshape(-1)[:, None] == jnp.arange(experts, dtype=jnp.int32)[None, :]
    ).astype(jnp.int32)
    before = jnp.cumsum(onehot, axis=0) - onehot
    slot_ids = jnp.sum(before * onehot, axis=1).reshape(rows_here, top_count)
    targets = expert_ids * capacity + slot_ids
    all_slots = jnp.arange(experts * capacity, dtype=jnp.int32)
    matches = all_slots[:, None, None] == targets[None, :, :]
    placing = jnp.any(matches, axis=2).astype(jnp.bfloat16)
    scaled = gate_weights * tok_weight[:, None]
    slot_scale = jnp.sum(jnp.where(matches, scaled[None, :, :], 0.0), axis=(1, 2))
    combining = jnp.sum(jnp.where(matches, gate_weights[None, :, :], 0.0), axis=2)
    wide_hidden = hidden.astype(jnp.float32)
    squares = lax.psum(jnp.sum(wide_hidden * wide_hidden, axis=1), "tp")
    scaling = lax.rsqrt(squares / width + 1e-05)
    normed = (wide_hidden * scaling[:, None] * gain.astype(jnp.float32)[None, :]).astype(
        jnp.bfloat16
    )
    block_rows = jnp.dot(placing, normed, preferred_element_type=jnp.float32).astype(jnp.bfloat16)
    block_cot = jnp.dot(placing, upstream, preferred_element_type=jnp.float32) * slot_scale[:, None]
    block_rows = block_rows.reshape(experts, capacity, -1)
    block_cot = block_cot.astype(jnp.bfloat16).reshape(experts, capacity, -1)
    came_rows, came_cot = (
        lax.all_to_all(block_rows, "tok", split_axis=0, concat_axis=0, tiled=True),
        lax.all_to_all(block_cot, "tok", split_axis=0, concat_axis=0, tiled=True),
    )
    part_rows, part_cot = (
        lax.all_gather(came_rows, "tp", axis=2, tiled=True),
        lax.all_gather(came_cot, "tp", axis=2, tiled=True),
    )
    pooled_rows, pooled_cot = (
        lax.all_gather(part_rows, "grp", axis=0, tiled=True),
        lax.all_gather(part_cot, "grp", axis=0, tiled=True),
    )
    rows_in = pooled_rows.reshape(-1, width)
    cot_in = pooled_cot.reshape(-1, width)
    gate_mat = w_gate[0]
    up_mat = w_up[0]
    down_mat = w_down[0]
    hidden_act, scores = expert_pass(rows_in, cot_in, gate_mat, up_mat, down_mat)
    importance = scores / (rows_here * experts * groups)
    partial_value = lax.psum_scatter(
        lax.dot_general(
            down_mat, hidden_act, (((0,), (1,)), ((), ())), preferred_element_type=jnp.float32
        ).astype(jnp.bfloat16),
        "tp",
        scatter_dimension=0,
        tiled=True,
    )
    summed = lax.psum_scatter(partial_value, "grp", scatter_dimension=1, tiled=True).astype(
        jnp.float32
    )
    slice_width = summed.shape[0]
    outgoing = summed.astype(jnp.bfloat16).reshape(slice_width, experts, capacity)
    returned = lax.all_to_all(outgoing, "tok", split_axis=1, concat_axis=1, tiled=True)
    returned = returned.reshape(slice_width, experts * capacity).astype(jnp.float32)
    combined = lax.dot_general(
        combining,
        returned,
        (((0,), (1,)), ((), ())),
        precision=lax.Precision.HIGHEST,
        preferred_element_type=jnp.float32,
    )
    mixed = (hidden.astype(jnp.float32) + combined).astype(jnp.bfloat16)
    return (mixed, importance[None, :])


def solution(mesh):
    placed = (
        P(("tok", "grp"), "tp"),
        P("tp"),
        P(("tok", "grp"), None),
        P(("tok", "grp"), None),
        P(("tok", "grp")),
        P(("tok", "grp"), "tp"),
        P("tok", None, ("tp", "grp")),
        P("tok", None, ("tp", "grp")),
        P("tok", ("tp", "grp"), None),
    )
    return jax.shard_map(
        on_device,
        mesh=mesh,
        in_specs=placed,
        out_specs=(P(("tok", "grp"), "tp"), P("tok", ("tp", "grp"))),
        check_vma=False,
    )
```

profile of v0, /device:TPU:1, one launch (start us, length us, event | category | flops | bytes accessed | tf_op | source)
XLA Modules:
  0.0 378.7 jit_solution(2218602018310981666)
XLA Ops:
  8.5 1.0 fusion.19
  9.5 34.2 %psum.14 = f32[128]{0:T(128)S(1)} all-reduce(f32[128]{0:T(128)S(1)} %fusion.19), channel_id=1, replica_groups=mesh['tok'=8,'tp'=16,'grp'=2] {'tp'}, use_global_device_ids=true, to_apply=%region_6.7 | all-reduce | flops 128 | bytes 1024 | tf_op jit(solution)/shard_map/psum | solution.py:60
  46.3 1.2 convolution_convert_fusion.1
  47.5 17.2 %all_to_all.15 = bf16[8,40,384]{2,1,0:T(8,128)(2,1)} all-to-all(bf16[8,40,384]{2,1,0:T(8,128)(2,1)S(1)} %bitcast.56), channel_id=1, replica_groups=mesh['tok'=8,'tp'=16,'grp'=2] {'tok'}, dimensions={0} | all-to-all | bytes 491520 | tf_op jit(solution)/shard_map/all_to_all | solution.py:70
  65.6 32.2 %psum.15 = f32[16]{0:T(128)S(1)} all-reduce(f32[16]{0:T(128)S(1)} %convert_reduce_fusion), channel_id=1, replica_groups=mesh['tok'=8,'tp'=16,'grp'=2] {'tok','grp'}, use_global_device_ids=true, to_apply=%region_10.11 | all-reduce | flops 16 | bytes 128 | tf_op jit(solution)/shard_map/psum | solution.py:44
  99.2 1.5 select_reduce_fusion
  101.0 12.8 %all_to_all.16 = bf16[8,40,384]{2,1,0:T(8,128)(2,1)} all-to-all(bf16[8,40,384]{2,1,0:T(8,128)(2,1)S(1)} %bitcast.57), channel_id=1, replica_groups=mesh['tok'=8,'tp'=16,'grp'=2] {'tok'}, dimensions={0} | all-to-all | bytes 491520 | tf_op jit(solution)/shard_map/all_to_all | solution.py:71
  113.8 10.2 %all-gather.5.cloned.1.call-done = bf16[8,40,6144]{2,1,0:T(8,128)(2,1)} async-done(((bf16[8,40,384]{2,1,0:T(8,128)(2,1)}), bf16[8,40,6144]{2,1,0:T(8,128)(2,1)}) %all-gather.5.cloned.1.call-update) | async-done | bytes 3932176 | tf_op jit(solution)/shard_map/all_gather | solution.py:74
  124.1 62.4 %all-gather.9.cloned.1.call-done = bf16[8,40,6144]{2,1,0:T(8,128)(2,1)} async-done(((bf16[8,40,384]{2,1,0:T(8,128)(2,1)}), bf16[8,40,6144]{2,1,0:T(8,128)(2,1)}) %all-gather.9.cloned.1.call-update) | async-done | bytes 3932176 | tf_op jit(solution)/shard_map/all_gather | solution.py:75
  186.5 27.7 %all-gather.7.cloned.1.call-done = bf16[16,40,6144]{2,1,0:T(8,128)(2,1)} async-done(((bf16[8,40,6144]{2,1,0:T(8,128)(2,1)}), bf16[16,40,6144]{2,1,0:T(8,128)(2,1)}) %all-gather.7.cloned.1.call-update) | async-done | bytes 7864336 | tf_op jit(solution)/shard_map/all_gather | solution.py:78
  214.2 5.6 %fusion.9 = f32[640,256]{1,0:T(8,128)S(1)} fusion(bf16[640,6144]{1,0:T(8,128)(2,1)} %bitcast.60, bf16[1,6144,256]{2,1,0:T(8,128)(2,1)S(1)} %copy-done.4), kind=kOutput, calls=%fused_computation.13 | convolution fusion | flops 2013265920 | bytes 11665408 | tf_op jit(solution)/shard_map/dot_general | solution.py:8
  220.6 3.0 multiply_convert_fusion.2
  224.4 6.1 %fusion = bf16[6144,640]{0,1:T(8,128)(2,1)} fusion(bf16[640,256]{1,0:T(8,128)(2,1)S(1)} %get-tuple-element.4, bf16[1,256,6144]{2,1,0:T(8,128)(2,1)S(1)} %copy-done.1), kind=kOutput, calls=%fused_computation.1 | convolution fusion | flops 2017198080 | bytes 11337728 | tf_op jit(solution)/shard_map/dot_general | solution.py:89
  230.5 10.7 %copy.34 = bf16[6144,640]{1,0:T(8,128)(2,1)} copy(bf16[6144,640]{0,1:T(8,128)(2,1)} %fusion) | data formatting | bytes 15728640
  241.6 5.6 %fusion.4 = f32[640,256]{1,0:T(8,128)S(1)} fusion(bf16[640,6144]{1,0:T(8,128)(2,1)} %bitcast.53, bf16[1,256,6144]{2,1,0:T(8,128)(2,1)S(1)} %copy-done.1), kind=kOutput, calls=%fused_computation.8 | convolution fusion | flops 2013265920 | bytes 11665408 | tf_op jit(solution)/shard_map/dot_general | solution.py:13
  248.1 6.2 %fusion.11 = f32[256]{0:T(256)S(1)} fusion(bf16[1,6144,256]{2,1,0:T(8,128)(2,1)S(1)} %copy-done.5, bf16[640,6144]{1,0:T(8,128)(2,1)} %bitcast.61, f32[640,256]{1,0:T(8,128)S(1)} %copy-done.8, f32[640,256]{1,0:T(8,128)S(1)} %fusion.4, f32[640,256]{1,0:T(8,128)S(1)} %copy-done.10), kind=kOutput, calls=%fused_computation.15 | convolution fusion | flops 2021195520 | bytes 12977152 | tf_op jit(solution)/shard_map/dot_general | solution.py:20
  254.3 80.1 %reduce-scatter.7.cloned.1.call-done = bf16[384,640]{1,0:T(8,128)(2,1)} async-done(((bf16[6144,640]{1,0:T(8,128)(2,1)}), bf16[384,640]{1,0:T(8,128)(2,1)}) %reduce-scatter.7.cloned.1.call-update) | async-done | bytes 491536
  334.4 2.0 copy.35
  336.5 7.4 %fusion.12 = f32[256]{0:T(256)S(1)} fusion(bf16[1,6144,256]{2,1,0:T(8,128)(2,1)} %param.16, bf16[640,6144]{1,0:T(8,128)(2,1)} %bitcast.62, f32[640,256]{1,0:T(8,128)} %copy-done.9, f32[640,256]{1,0:T(8,128)} %copy-done.7), kind=kOutput, calls=%fused_computation.16 | convolution fusion | flops 2020540160 | bytes 12321792 | tf_op jit(solution)/shard_map/dot_general | solution.py:23
  343.8 7.7 %reduce-scatter.5.cloned.1.call-done = bf16[384,320]{0,1:T(8,128)(2,1)} async-done(((bf16[384,640]{0,1:T(8,128)(2,1)}), bf16[384,320]{0,1:T(8,128)(2,1)}) %reduce-scatter.5.cloned.1.call-update) | async-done | bytes 245776 | tf_op jit(solution)/shard_map/reduce_scatter | solution.py:96
  351.5 6.5 %all-to-all-start.1 = ((bf16[384,8,40]{0,2,1:T(8,128)(2,1)}), bf16[384,8,40]{0,2,1:T(8,128)(2,1)S(1)}, u32[]{:S(2)}, u32[]{:S(2)}) async-start(bf16[384,8,40]{0,2,1:T(8,128)(2,1)} %bitcast.58), calls=%async_computation.2 | async-start | bytes 491520 | tf_op jit(solution)/shard_map/all_to_all | solution.py:101
  358.0 6.5 %fusion.13 = f32[256]{0:T(256)S(1)} fusion(bf16[1,256,6144]{2,1,0:T(8,128)(2,1)S(1)} %copy-done.1, bf16[640,256]{1,0:T(8,128)(2,1)} %copy-done.2, bf16[640,6144]{1,0:T(8,128)(2,1)} %bitcast.54), kind=kOutput, calls=%fused_computation.17 | convolution fusion | flops 2019557120 | bytes 11338752 | tf_op jit(solution)/shard_map/dot_general | solution.py:26
  365.0 4.8 %all-to-all-done.1 = bf16[384,8,40]{0,2,1:T(8,128)(2,1)S(1)} async-done(((bf16[384,8,40]{0,2,1:T(8,128)(2,1)}), bf16[384,8,40]{0,2,1:T(8,128)(2,1)S(1)}, u32[]{:S(2)}, u32[]{:S(2)}) %all-to-all-start.1) | async-done | bytes 245792 | tf_op jit(solution)/shard_map/all_to_all | solution.py:101
  369.8 2.0 fusion.15
  (56 shorter events, 9.8 us)
Async XLA Ops:
  7.2 93.6 %copy-start = (bf16[128,384]{1,0:T(8,128)(2,1)S(1)}, bf16[128,384]{1,0:T(8,128)(2,1)}, u32[]{:S(2)}) copy-start(bf16[128,384]{1,0:T(8,128)(2,1)} %param.14) | copy-start | bytes 294916
  7.2 207.0 %copy-start.4 = (bf16[1,6144,256]{2,1,0:T(8,128)(2,1)S(1)}, bf16[1,6144,256]{2,1,0:T(8,128)(2,1)}, u32[]{:S(2)}) copy-start(bf16[1,6144,256]{2,1,0:T(8,128)(2,1)} %param.15) | copy-start | bytes 9437188
  7.2 116.8 %all-gather.5.cloned.1.call-start = ((), (), s32[]{:S(2)}) async-start(), calls=%async_computation.5 | async-start | bytes 4177920 | tf_op jit(solution)/shard_map/all_gather | solution.py:74
  64.7 121.7 %all-gather.9.cloned.1.call-start = ((), (), s32[]{:S(2)}) async-start(), calls=%async_computation.8 | async-start | bytes 4177920 | tf_op jit(solution)/shard_map/all_gather | solution.py:75
  113.8 100.4 %all-gather.7.cloned.1.call-start = ((), (), s32[]{:S(2)}) async-start(), calls=%async_computation.6 | async-start | bytes 11796480 | tf_op jit(solution)/shard_map/all_gather | solution.py:78
  124.1 117.6 %all-gather.11.cloned.1.call-start = ((), (), s32[]{:S(2)}) async-start(), calls=%async_computation.9 | async-start | bytes 11796480 | tf_op jit(solution)/shard_map/all_gather | solution.py:79
  186.5 147.9 %reduce-scatter.7.cloned.1.call-start = ((), (), s32[]{:S(2)}) async-start(), calls=%async_computation.10 | async-start | bytes 8355840
  214.2 5.6 %copy-start.3 = (bf16[16,40,6144]{2,1,0:T(8,128)(2,1)S(1)}, bf16[16,40,6144]{2,1,0:T(8,128)(2,1)}, u32[]{:S(2)}) copy-start(bf16[16,40,6144]{2,1,0:T(8,128)(2,1)} %all-gather.7.cloned.1.call-done) | copy-start | bytes 23592964
  214.2 6.4 %copy-start.6 = (bf16[1,6144,256]{2,1,0:T(8,128)(2,1)S(1)}, bf16[1,6144,256]{2,1,0:T(8,128)(2,1)}, u32[]{:S(2)}) copy-start(bf16[1,6144,256]{2,1,0:T(8,128)(2,1)} %param.16) | copy-start | bytes 9437188
  220.6 3.0 copy-start.7
  220.6 3.8 copy-start.1
  223.6 0.7 copy-start.2
  241.2 110.2 %reduce-scatter.5.cloned.1.call-start = ((), (), s32[]{:S(2)}) async-start(), calls=%async_computation.7 | async-start | bytes 737280 | tf_op jit(solution)/shard_map/reduce_scatter | solution.py:96
  241.6 6.5 %copy-start.5 = (bf16[1,6144,256]{2,1,0:T(8,128)(2,1)S(1)}, bf16[1,6144,256]{2,1,0:T(8,128)(2,1)}, u32[]{:S(2)}) copy-start(bf16[1,6144,256]{2,1,0:T(8,128)(2,1)} %param.15) | copy-start | bytes 9437188
  241.6 6.5 %copy-start.8 = (f32[640,256]{1,0:T(8,128)S(1)}, f32[640,256]{1,0:T(8,128)}, u32[]{:S(2)}) copy-start(f32[640,256]{1,0:T(8,128)} %copy-done.7) | copy-start | bytes 1966084
  241.6 6.5 %copy-start.10 = (f32[640,256]{1,0:T(8,128)S(1)}, f32[640,256]{1,0:T(8,128)}, u32[]{:S(2)}) copy-start(f32[640,256]{1,0:T(8,128)} %get-tuple-element.5) | copy-start | bytes 1966084
  247.2 0.8 copy-start.9
  351.5 18.3 %all-to-all-start.1 = ((bf16[384,8,40]{0,2,1:T(8,128)(2,1)}), bf16[384,8,40]{0,2,1:T(8,128)(2,1)S(1)}, u32[]{:S(2)}, u32[]{:S(2)}) async-start(bf16[384,8,40]{0,2,1:T(8,128)(2,1)} %bitcast.58), calls=%async_computation.2 | async-start | bytes 491520 | tf_op jit(solution)/shard_map/all_to_all | solution.py:101
Sparse Core Ops, SparseCore 0:
  64.9 59.1 all-gather.4
  126.4 59.9 all-gather.8
  188.3 25.9 all-gather.6
  215.9 25.6 all-gather.10
  245.3 89.1 reduce-scatter.6
  336.8 14.6 reduce-scatter.4
where the time goes:
time: 379 us
  waiting for transfers between devices  193 us (51%)
  blocking collectives  96.5 us (25%)
  matrix products  43.9 us (12%)
  local copies, waits for them, and re-layouts  16.8 us (4%)
  between operations  14.2 us (4%)
  other arithmetic  7.42 us (2%)
  starting transfers between devices  6.89 us (2%)
    unnamed x7, waiting for transfers between devices  80.2 us
    all_gather x1, waiting for transfers between devices, on_device(): lax.all_gather(came_cot, 'tp', axis=2, tiled=True)  62.4 us
    psum x1, blocking collectives, on_device(): squares = lax.psum(jnp.sum(wide_hidden * wide_hidden, axis=1), 'tp')  34.2 us
    psum x1, blocking collectives, on_device(): doc_len = lax.psum(jnp.sum(doc_onehot, axis=0), ('tok', 'grp'))  32.2 us
    all_gather x1, waiting for transfers between devices, on_device(): lax.all_gather(part_rows, 'grp', axis=0, tiled=True)  27.7 us
    all_to_all x1, blocking collectives, on_device(): lax.all_to_all(block_rows, 'tok', split_axis=0, concat_axis=0, tiled=True)  17.2 us
    unnamed x25, local copies, waits for them, and re-layouts  16.1 us
    all_to_all x1, blocking collectives, on_device(): lax.all_to_all(block_cot, 'tok', split_axis=0, concat_axis=0, tiled=True)  12.8 us
  transfers between devices with their start and end apart: 7, of which 7 were waited for; matrix products, arithmetic and copies ran while one was open for 15% of the time, Pallas kernels for 0%

commit v1 on v0

--- a/solution.py
+++ b/solution.py
@@ -57,7 +57,7 @@
     slot_scale = jnp.sum(jnp.where(matches, scaled[None, :, :], 0.0), axis=(1, 2))
     combining = jnp.sum(jnp.where(matches, gate_weights[None, :, :], 0.0), axis=2)
     wide_hidden = hidden.astype(jnp.float32)
-    squares = lax.psum(jnp.sum(wide_hidden * wide_hidden, axis=1), "tp")
+    squares = jnp.sum(lax.all_gather(jnp.sum(wide_hidden * wide_hidden, axis=1), "tp"), axis=0)
     scaling = lax.rsqrt(squares / width + 1e-05)
     normed = (wide_hidden * scaling[:, None] * gain.astype(jnp.float32)[None, :]).astype(
         jnp.bfloat16

time: 379 us -> 363 us (0.958)
  blocking collectives: 96.5 us -> 79.3 us
    psum x1 -> x0, blocking collectives: 34.2 us -> none  [on_device(): squares = lax.psum(jnp.sum(wide_hidden * wide_hidden, axis=1), 'tp')]
    all_gather x0 -> x1, blocking collectives: none -> 17.2 us  [on_device(): lax.all_gather(jnp.sum(wide_hidden * wide_hidden, axis=1), 'tp')]
where the time goes in v1:
time: 363 us
  waiting for transfers between devices  194 us (53%)
  blocking collectives  79.3 us (22%)
  matrix products  43.9 us (12%)
  local copies, waits for them, and re-layouts  16.8 us (5%)
  between operations  14.2 us (4%)
  other arithmetic  7.48 us (2%)
  starting transfers between devices  6.89 us (2%)
    unnamed x7, waiting for transfers between devices  80.4 us
    all_gather x1, waiting for transfers between devices, on_device(): lax.all_gather(came_cot, 'tp', axis=2, tiled=True)  62.4 us
    psum x1, blocking collectives, on_device(): doc_len = lax.psum(jnp.sum(doc_onehot, axis=0), ('tok', 'grp'))  29.9 us
    all_gather x1, waiting for transfers between devices, on_device(): lax.all_gather(part_rows, 'grp', axis=0, tiled=True)  27.7 us
    all_to_all x1, blocking collectives, on_device(): lax.all_to_all(block_rows, 'tok', split_axis=0, concat_axis=0, tiled=True)  17.2 us
    all_gather x1, blocking collectives, on_device(): lax.all_gather(jnp.sum(wide_hidden * wide_hidden, axis=1), 'tp')  17.2 us
    unnamed x25, local copies, waits for them, and re-layouts  16.1 us
    all_to_all x1, blocking collectives, on_device(): lax.all_to_all(block_cot, 'tok', split_axis=0, concat_axis=0, tiled=True)  15 us
  transfers between devices with their start and end apart: 7, of which 7 were waited for; matrix products, arithmetic and copies ran while one was open for 15% of the time, Pallas kernels for 0%

profile of v1, /device:TPU:1, one launch (start us, length us, event | category | flops | bytes accessed | tf_op | source)
XLA Modules:
  0.0 362.6 jit_solution(11167888134111405013)
XLA Ops:
  8.5 1.0 fusion.19
  10.2 17.2 %all-gather.1 = f32[16,1,128]{2,1,0:T(1,128)S(1)} all-gather(f32[1,1,128]{2,1,0:T(1,128)S(1)} %bitcast.60), channel_id=2, replica_groups=mesh['tok'=8,'tp'=16,'grp'=2] {'tp'}, dimensions={0}, use_global_device_ids=true | all-gather | bytes 8704 | tf_op jit(solution)/shard_map/all_gather | solution.py:60
  29.3 1.2 convolution_convert_fusion.1
  30.4 17.2 %all_to_all.15 = bf16[8,40,384]{2,1,0:T(8,128)(2,1)} all-to-all(bf16[8,40,384]{2,1,0:T(8,128)(2,1)S(1)} %bitcast.57), channel_id=1, replica_groups=mesh['tok'=8,'tp'=16,'grp'=2] {'tok'}, dimensions={0} | all-to-all | bytes 491520 | tf_op jit(solution)/shard_map/all_to_all | solution.py:70
  48.5 29.9 %psum.7 = f32[16]{0:T(128)S(1)} all-reduce(f32[16]{0:T(128)S(1)} %convert_reduce_fusion), channel_id=1, replica_groups=mesh['tok'=8,'tp'=16,'grp'=2] {'tok','grp'}, use_global_device_ids=true, to_apply=%region_10.11 | all-reduce | flops 16 | bytes 128 | tf_op jit(solution)/shard_map/psum | solution.py:44
  79.9 1.5 select_reduce_fusion
  81.6 15.0 %all_to_all.16 = bf16[8,40,384]{2,1,0:T(8,128)(2,1)} all-to-all(bf16[8,40,384]{2,1,0:T(8,128)(2,1)S(1)} %bitcast.58), channel_id=1, replica_groups=mesh['tok'=8,'tp'=16,'grp'=2] {'tok'}, dimensions={0} | all-to-all | bytes 491520 | tf_op jit(solution)/shard_map/all_to_all | solution.py:71
  96.7 11.0 %all-gather.7.cloned.1.call-done = bf16[8,40,6144]{2,1,0:T(8,128)(2,1)} async-done(((bf16[8,40,384]{2,1,0:T(8,128)(2,1)}), bf16[8,40,6144]{2,1,0:T(8,128)(2,1)}) %all-gather.7.cloned.1.call-update) | async-done | bytes 3932176 | tf_op jit(solution)/shard_map/all_gather | solution.py:74
  107.8 62.4 %all-gather.11.cloned.1.call-done = bf16[8,40,6144]{2,1,0:T(8,128)(2,1)} async-done(((bf16[8,40,384]{2,1,0:T(8,128)(2,1)}), bf16[8,40,6144]{2,1,0:T(8,128)(2,1)}) %all-gather.11.cloned.1.call-update) | async-done | bytes 3932176 | tf_op jit(solution)/shard_map/all_gather | solution.py:75
  170.2 27.7 %all-gather.9.cloned.1.call-done = bf16[16,40,6144]{2,1,0:T(8,128)(2,1)} async-done(((bf16[8,40,6144]{2,1,0:T(8,128)(2,1)}), bf16[16,40,6144]{2,1,0:T(8,128)(2,1)}) %all-gather.9.cloned.1.call-update) | async-done | bytes 7864336 | tf_op jit(solution)/shard_map/all_gather | solution.py:78
  197.9 5.6 %fusion.9 = f32[640,256]{1,0:T(8,128)S(1)} fusion(bf16[640,6144]{1,0:T(8,128)(2,1)} %bitcast.62, bf16[1,6144,256]{2,1,0:T(8,128)(2,1)S(1)} %copy-done.4), kind=kOutput, calls=%fused_computation.13 | convolution fusion | flops 2013265920 | bytes 11665408 | tf_op jit(solution)/shard_map/dot_general | solution.py:8
  204.2 3.0 multiply_convert_fusion.2
  208.0 6.1 %fusion = bf16[6144,640]{0,1:T(8,128)(2,1)} fusion(bf16[640,256]{1,0:T(8,128)(2,1)S(1)} %get-tuple-element.4, bf16[1,256,6144]{2,1,0:T(8,128)(2,1)S(1)} %copy-done.1), kind=kOutput, calls=%fused_computation.1 | convolution fusion | flops 2017198080 | bytes 11337728 | tf_op jit(solution)/shard_map/dot_general | solution.py:89
  214.1 10.7 %copy.34 = bf16[6144,640]{1,0:T(8,128)(2,1)} copy(bf16[6144,640]{0,1:T(8,128)(2,1)} %fusion) | data formatting | bytes 15728640
  225.3 5.6 %fusion.4 = f32[640,256]{1,0:T(8,128)S(1)} fusion(bf16[640,6144]{1,0:T(8,128)(2,1)} %bitcast.54, bf16[1,256,6144]{2,1,0:T(8,128)(2,1)S(1)} %copy-done.1), kind=kOutput, calls=%fused_computation.8 | convolution fusion | flops 2013265920 | bytes 11665408 | tf_op jit(solution)/shard_map/dot_general | solution.py:13
  231.7 6.2 %fusion.11 = f32[256]{0:T(256)S(1)} fusion(bf16[1,6144,256]{2,1,0:T(8,128)(2,1)S(1)} %copy-done.5, bf16[640,6144]{1,0:T(8,128)(2,1)} %bitcast.63, f32[640,256]{1,0:T(8,128)S(1)} %copy-done.8, f32[640,256]{1,0:T(8,128)S(1)} %fusion.4, f32[640,256]{1,0:T(8,128)S(1)} %copy-done.10), kind=kOutput, calls=%fused_computation.15 | convolution fusion | flops 2021195520 | bytes 12977152 | tf_op jit(solution)/shard_map/dot_general | solution.py:20
  238.0 80.3 %reduce-scatter.7.cloned.1.call-done = bf16[384,640]{1,0:T(8,128)(2,1)} async-done(((bf16[6144,640]{1,0:T(8,128)(2,1)}), bf16[384,640]{1,0:T(8,128)(2,1)}) %reduce-scatter.7.cloned.1.call-update) | async-done | bytes 491536
  318.2 2.0 copy.35
  320.3 7.4 %fusion.12 = f32[256]{0:T(256)S(1)} fusion(bf16[1,6144,256]{2,1,0:T(8,128)(2,1)} %param.16, bf16[640,6144]{1,0:T(8,128)(2,1)} %bitcast.64, f32[640,256]{1,0:T(8,128)} %copy-done.9, f32[640,256]{1,0:T(8,128)} %copy-done.7), kind=kOutput, calls=%fused_computation.16 | convolution fusion | flops 2020540160 | bytes 12321792 | tf_op jit(solution)/shard_map/dot_general | solution.py:23
  327.6 7.7 %reduce-scatter.5.cloned.1.call-done = bf16[384,320]{0,1:T(8,128)(2,1)} async-done(((bf16[384,640]{0,1:T(8,128)(2,1)}), bf16[384,320]{0,1:T(8,128)(2,1)}) %reduce-scatter.5.cloned.1.call-update) | async-done | bytes 245776 | tf_op jit(solution)/shard_map/reduce_scatter | solution.py:96
  335.4 6.5 %all-to-all-start.1 = ((bf16[384,8,40]{0,2,1:T(8,128)(2,1)}), bf16[384,8,40]{0,2,1:T(8,128)(2,1)S(1)}, u32[]{:S(2)}, u32[]{:S(2)}) async-start(bf16[384,8,40]{0,2,1:T(8,128)(2,1)} %bitcast.59), calls=%async_computation.2 | async-start | bytes 491520 | tf_op jit(solution)/shard_map/all_to_all | solution.py:101
  341.8 6.5 %fusion.13 = f32[256]{0:T(256)S(1)} fusion(bf16[1,256,6144]{2,1,0:T(8,128)(2,1)S(1)} %copy-done.1, bf16[640,256]{1,0:T(8,128)(2,1)} %copy-done.2, bf16[640,6144]{1,0:T(8,128)(2,1)} %bitcast.55), kind=kOutput, calls=%fused_computation.17 | convolution fusion | flops 2019557120 | bytes 11338752 | tf_op jit(solution)/shard_map/dot_general | solution.py:26
  348.9 4.8 %all-to-all-done.1 = bf16[384,8,40]{0,2,1:T(8,128)(2,1)S(1)} async-done(((bf16[384,8,40]{0,2,1:T(8,128)(2,1)}), bf16[384,8,40]{0,2,1:T(8,128)(2,1)S(1)}, u32[]{:S(2)}, u32[]{:S(2)}) %all-to-all-start.1) | async-done | bytes 245792 | tf_op jit(solution)/shard_map/all_to_all | solution.py:101
  353.7 2.0 fusion.15
  (57 shorter events, 9.9 us)
Async XLA Ops:
  7.2 74.2 %copy-start = (bf16[128,384]{1,0:T(8,128)(2,1)S(1)}, bf16[128,384]{1,0:T(8,128)(2,1)}, u32[]{:S(2)}) copy-start(bf16[128,384]{1,0:T(8,128)(2,1)} %param.14) | copy-start | bytes 294916
  7.2 190.7 %copy-start.4 = (bf16[1,6144,256]{2,1,0:T(8,128)(2,1)S(1)}, bf16[1,6144,256]{2,1,0:T(8,128)(2,1)}, u32[]{:S(2)}) copy-start(bf16[1,6144,256]{2,1,0:T(8,128)(2,1)} %param.15) | copy-start | bytes 9437188
  7.2 100.5 %all-gather.7.cloned.1.call-start = ((), (), s32[]{:S(2)}) async-start(), calls=%async_computation.5 | async-start | bytes 4177920 | tf_op jit(solution)/shard_map/all_gather | solution.py:74
  47.7 122.4 %all-gather.11.cloned.1.call-start = ((), (), s32[]{:S(2)}) async-start(), calls=%async_computation.8 | async-start | bytes 4177920 | tf_op jit(solution)/shard_map/all_gather | solution.py:75
  96.7 101.2 %all-gather.9.cloned.1.call-start = ((), (), s32[]{:S(2)}) async-start(), calls=%async_computation.6 | async-start | bytes 11796480 | tf_op jit(solution)/shard_map/all_gather | solution.py:78
  107.7 117.6 %all-gather.13.cloned.1.call-start = ((), (), s32[]{:S(2)}) async-start(), calls=%async_computation.9 | async-start | bytes 11796480 | tf_op jit(solution)/shard_map/all_gather | solution.py:79
  170.1 148.1 %reduce-scatter.7.cloned.1.call-start = ((), (), s32[]{:S(2)}) async-start(), calls=%async_computation.10 | async-start | bytes 8355840
  197.9 5.6 %copy-start.3 = (bf16[16,40,6144]{2,1,0:T(8,128)(2,1)S(1)}, bf16[16,40,6144]{2,1,0:T(8,128)(2,1)}, u32[]{:S(2)}) copy-start(bf16[16,40,6144]{2,1,0:T(8,128)(2,1)} %all-gather.9.cloned.1.call-done) | copy-start | bytes 23592964
  197.9 6.4 %copy-start.6 = (bf16[1,6144,256]{2,1,0:T(8,128)(2,1)S(1)}, bf16[1,6144,256]{2,1,0:T(8,128)(2,1)}, u32[]{:S(2)}) copy-start(bf16[1,6144,256]{2,1,0:T(8,128)(2,1)} %param.16) | copy-start | bytes 9437188
  204.2 3.0 copy-start.7
  204.2 3.8 %copy-start.1 = (bf16[1,256,6144]{2,1,0:T(8,128)(2,1)S(1)}, bf16[1,256,6144]{2,1,0:T(8,128)(2,1)}, u32[]{:S(2)}) copy-start(bf16[1,256,6144]{2,1,0:T(8,128)(2,1)} %param.17) | copy-start | bytes 9437188
  207.3 0.7 copy-start.2
  224.9 110.5 %reduce-scatter.5.cloned.1.call-start = ((), (), s32[]{:S(2)}) async-start(), calls=%async_computation.7 | async-start | bytes 737280 | tf_op jit(solution)/shard_map/reduce_scatter | solution.py:96
  225.3 6.5 %copy-start.5 = (bf16[1,6144,256]{2,1,0:T(8,128)(2,1)S(1)}, bf16[1,6144,256]{2,1,0:T(8,128)(2,1)}, u32[]{:S(2)}) copy-start(bf16[1,6144,256]{2,1,0:T(8,128)(2,1)} %param.15) | copy-start | bytes 9437188
  225.3 6.5 %copy-start.8 = (f32[640,256]{1,0:T(8,128)S(1)}, f32[640,256]{1,0:T(8,128)}, u32[]{:S(2)}) copy-start(f32[640,256]{1,0:T(8,128)} %copy-done.7) | copy-start | bytes 1966084
  225.3 6.5 %copy-start.10 = (f32[640,256]{1,0:T(8,128)S(1)}, f32[640,256]{1,0:T(8,128)}, u32[]{:S(2)}) copy-start(f32[640,256]{1,0:T(8,128)} %get-tuple-element.5) | copy-start | bytes 1966084
  230.9 0.8 copy-start.9
  335.4 18.3 %all-to-all-start.1 = ((bf16[384,8,40]{0,2,1:T(8,128)(2,1)}), bf16[384,8,40]{0,2,1:T(8,128)(2,1)S(1)}, u32[]{:S(2)}, u32[]{:S(2)}) async-start(bf16[384,8,40]{0,2,1:T(8,128)(2,1)} %bitcast.59), calls=%async_computation.2 | async-start | bytes 491520 | tf_op jit(solution)/shard_map/all_to_all | solution.py:101
Sparse Core Ops, SparseCore 0:
  47.8 59.8 all-gather.6
  110.1 59.9 all-gather.10
  171.9 25.9 all-gather.8
  199.5 25.6 all-gather.12
  228.9 89.2 reduce-scatter.6
  320.6 14.6 reduce-scatter.4
